TPU v7x, 32 devices: a whole 2x2x4 slice. The times are simulated.
32 devices in a mesh: dp: 2 (over x), expert: 16 (over z, y, core).
Axes of the slice: x: 2, y: 2, z: 4, core: 2. Of those that a mesh axis runs over, the one named last changes fastest.
Arguments:
- tokens: bfloat16 [512, 2048], P('expert', 'dp'), may hold values from -6 to 6
- cotangent: bfloat16 [512, 2048], P('expert', 'dp'), may hold values from -6 to 6
- routes: int32 [512, 8], P('expert'), may hold values from 0 to 15, all different within a row; in each aligned block of 32 rows (0 to 31, 32 to 63, ...) at most 20 rows name the same one
- probs: float32 [512, 8], P('expert'), may hold values from 0.03 to 0.6
- matching: int32 [16], replicated, may hold values from 0 to 15, as said below
- gate_weight: bfloat16 [16, 2048, 1024], P('expert', None, 'dp'), may hold values from -0.125 to 0.125
- up_weight: bfloat16 [16, 2048, 1024], P('expert', None, 'dp'), may hold values from -0.125 to 0.125
- down_weight: bfloat16 [16, 2048, 1024], P('expert', None, 'dp'), may hold values from -0.1875 to 0.1875
Outputs:
- input_grad: bfloat16 [512, 2048], P('expert', 'dp')
- gate_weight_grad: float32 [16, 2048, 1024], P('expert', None, 'dp')
- up_weight_grad: float32 [16, 2048, 1024], P('expert', None, 'dp')
- down_weight_grad: float32 [16, 2048, 1024], P('expert', None, 'dp')
Inputs may be any that keep to these rules, and one draw needn't show every extreme that they name: matching pairs the experts: matching[matching[i]] == i and matching[i] != i. `routes`: each token names 8 different experts; within each aligned block of 32 tokens no expert is named by more than 20 tokens.
All inputs are finite; a program needn't handle non-finite values.
Results may differ from a plain program's by a relative error of at most 0.015.
Values may be sent and summed in bfloat16 or wider, within the bound.
A program may use at most 64 MiB of HBM per device.

v0:
```python
import jax
import jax.numpy as jnp
from jax import lax
from jax.sharding import PartitionSpec as P

contract_rows = (((0,), (0,)), ((), ()))
contract_cols = (((1,), (1,)), ((), ()))


def pair_rows(cotangent, routes, probs, expert):
    weight = jnp.sum(jnp.where(routes == expert, probs, 0.0), axis=1)
    return (cotangent.astype(jnp.float32) * weight[:, None]).astype(jnp.bfloat16)


def local(tokens, cotangent, routes, probs, matching, gate_weight, up_weight, down_weight):
    experts = matching.shape[0]
    tok_rows = routes.shape[0]
    hidden_width = gate_weight.shape[2]
    me = lax.axis_index("expert")
    w_gate, w_up, w_down = (gate_weight[0], up_weight[0], down_weight[0])
    routes_all = lax.all_gather(routes, "expert", axis=0, tiled=True)
    probs_all = lax.all_gather(probs, "expert", axis=0, tiled=True)
    both = jnp.stack([tokens, cotangent], axis=0)
    both = lax.all_gather(both, "dp", axis=2, tiled=True)
    both = lax.all_gather(both, "expert", axis=1, tiled=True)
    rows, cot = (both[0], both[1])
    grads = pair_rows(cot, routes_all, probs_all, me)
    gate = jnp.dot(rows, w_gate, preferred_element_type=jnp.float32)
    upper = jnp.dot(rows, w_up, preferred_element_type=jnp.float32)
    sig = jax.nn.sigmoid(gate)
    hidden = (gate * sig * upper).astype(jnp.bfloat16)
    hidden_back = jnp.dot(grads, w_down, preferred_element_type=jnp.float32)
    up_back = (hidden_back * gate * sig).astype(jnp.bfloat16)
    gate_back = (hidden_back * upper * sig * (1.0 + gate * (1.0 - sig))).astype(jnp.bfloat16)
    packed = jnp.concatenate([gate_back, up_back, hidden], axis=1)
    packed = packed.reshape(experts, tok_rows, 3 * hidden_width)
    spread = lax.all_to_all(packed, "expert", split_axis=0, concat_axis=0, tiled=True)
    ordered = jnp.take(spread, matching, axis=0)
    landed = lax.all_to_all(ordered, "expert", split_axis=0, concat_axis=0, tiled=True)
    landed = landed.reshape(experts * tok_rows, 3 * hidden_width)
    part = lax.dot_general(gate_back, w_gate, contract_cols, preferred_element_type=jnp.float32)
    part = part + lax.dot_general(up_back, w_up, contract_cols, preferred_element_type=jnp.float32)
    part = part.astype(jnp.bfloat16)
    summed = lax.psum_scatter(part, "dp", scatter_dimension=1, tiled=True)
    summed = summed.reshape(experts, tok_rows, summed.shape[1])
    back = lax.all_to_all(summed, "expert", split_axis=0, concat_axis=0, tiled=True)
    input_grad = jnp.sum(back.astype(jnp.float32), axis=0).astype(jnp.bfloat16)
    partner = matching[me]
    p_grads = pair_rows(cot, routes_all, probs_all, partner)
    g_gate = lax.dot_general(
        rows, landed[:, :hidden_width], contract_rows, preferred_element_type=jnp.float32
    )
    g_up = lax.dot_general(
        rows,
        landed[:, hidden_width : 2 * hidden_width],
        contract_rows,
        preferred_element_type=jnp.float32,
    )
    g_down = lax.dot_general(
        p_grads, landed[:, 2 * hidden_width :], contract_rows, preferred_element_type=jnp.float32
    )
    return (input_grad, g_gate[None], g_up[None], g_down[None])


def solution(mesh):
    placed = (
        P("expert", "dp"),
        P("expert", "dp"),
        P("expert", None),
        P("expert", None),
        P(),
        P("expert", None, "dp"),
        P("expert", None, "dp"),
        P("expert", None, "dp"),
    )
    return jax.shard_map(
        local,
        mesh=mesh,
        in_specs=placed,
        out_specs=(
            P("expert", "dp"),
            P("expert", None, "dp"),
            P("expert", None, "dp"),
            P("expert", None, "dp"),
        ),
        check_vma=False,
    )
```

profile of v0, /device:TPU:9, one launch (start us, length us, event | category | flops | bytes accessed | tf_op | source)
XLA Modules:
  0.0 202.9 jit_solution(15081266872429991125)
XLA Ops:
  7.2 0.0 all-gather.4.cloned.1.call-start
  7.2 1.0 pad_maximum_fusion.1
  8.3 5.1 %all_gather.12 = bf16[2,32,2048]{2,1,0:T(8,128)(2,1)} all-gather(bf16[2,32,1024]{2,1,0:T(8,128)(2,1)S(1)} %pad_maximum_fusion.1), channel_id=1, replica_groups=mesh['dp'=2,'expert'=16] {'dp'}, dimensions={2}, use_global_device_ids=true | all-gather | bytes 393216 | tf_op jit(solution)/shard_map/all_gather | solution.py:24
  13.4 1.2 dynamic_slice.3
  14.7 20.8 %all-gather = s32[16,32,8]{1,2,0:T(8,128)S(1)} all-gather(s32[1,32,8]{1,2,0:T(8,128)} %bitcast.53), channel_id=1, replica_groups=mesh['dp'=2,'expert'=16] {'expert'}, dimensions={0}, use_global_device_ids=true | all-gather | bytes 17408 | tf_op jit(solution)/shard_map/all_gather | solution.py:21
  35.5 18.5 %all-gather.1 = f32[16,32,8]{1,2,0:T(8,128)S(1)} all-gather(f32[1,32,8]{1,2,0:T(8,128)} %bitcast.54), channel_id=1, replica_groups=mesh['dp'=2,'expert'=16] {'expert'}, dimensions={0}, use_global_device_ids=true | all-gather | bytes 17408 | tf_op jit(solution)/shard_map/all_gather | solution.py:22
  54.0 0.7 select_reduce_fusion
  54.7 0.1 reshape.57
  54.8 11.9 %all-gather.4.cloned.1.call-done = bf16[2,512,2048]{2,1,0:T(8,128)(2,1)} async-done(((bf16[2,32,2048]{2,1,0:T(8,128)(2,1)}), bf16[2,512,2048]{2,1,0:T(8,128)(2,1)}) %all-gather.4.cloned.1.call-update) | async-done | bytes 4194320 | tf_op jit(solution)/shard_map/all_gather | solution.py:25
  66.7 3.7 %fusion.9 = f32[512,512]{0,1:T(8,128)S(1)} fusion(bf16[1,2048,512]{2,1,0:T(8,128)(2,1)} %param.13, bf16[2,512,2048]{2,1,0:T(8,128)(2,1)} %all-gather.4.cloned.1.call-done), kind=kOutput, calls=%fused_computation.15 | convolution fusion | flops 1073741824 | bytes 5242880 | tf_op jit(solution)/shard_map/dot_general | solution.py:28
  70.3 0.4 copy-done.3
  70.8 1.4 fusion.5
  72.2 1.7 multiply_convert_fusion
  73.9 1.2 pad_maximum_fusion
  75.1 2.6 %copy.13 = bf16[512,1536]{1,0:T(8,128)(2,1)} copy(bf16[512,1536]{0,1:T(8,128)(2,1)} %pad_maximum_fusion) | data formatting | bytes 3145728 | tf_op jit(solution)/shard_map/concatenate | solution.py:35
  77.7 4.5 %all-to-all-start.1 = ((bf16[16,32,1536]{2,1,0:T(8,128)(2,1)}), bf16[16,32,1536]{2,1,0:T(8,128)(2,1)}, u32[]{:S(2)}, u32[]{:S(2)}) async-start(bf16[16,32,1536]{2,1,0:T(8,128)(2,1)} %bitcast.49), calls=%async_computation.2 | async-start | bytes 3145728 | tf_op jit(solution)/shard_map/all_to_all | solution.py:37
  82.2 0.0 reduce-scatter.2.cloned.1.call-start
  82.3 2.9 %fusion.7 = f32[512,2048]{1,0:T(8,128)S(1)} fusion(bf16[512,512]{0,1:T(8,128)(2,1)S(1)} %get-tuple-element.7, bf16[1,2048,512]{2,1,0:T(8,128)(2,1)} %param.13), kind=kOutput, calls=%fused_computation.13 | convolution fusion | flops 1073741824 | bytes 6815744 | tf_op jit(solution)/shard_map/dot_general | solution.py:41
  85.2 2.6 %add_convert_fusion = bf16[512,2048]{1,0:T(8,128)(2,1)} fusion(f32[512,2048]{1,0:T(8,128)S(1)} %fusion.7, bf16[512,512]{0,1:T(8,128)(2,1)S(1)} %get-tuple-element.8, bf16[1,2048,512]{2,1,0:T(8,128)(2,1)S(1)} %copy-done), kind=kOutput, calls=%fused_computation.6 | convolution fusion | flops 1075838976 | bytes 8912896 | tf_op jit(solution)/shard_map/dot_general | solution.py:42
  87.8 0.6 copy-done.4
  88.5 29.4 %all-to-all-done.1 = bf16[16,32,1536]{2,1,0:T(8,128)(2,1)} async-done(((bf16[16,32,1536]{2,1,0:T(8,128)(2,1)}), bf16[16,32,1536]{2,1,0:T(8,128)(2,1)}, u32[]{:S(2)}, u32[]{:S(2)}) %all-to-all-start.1) | async-done | bytes 1572896 | tf_op jit(solution)/shard_map/all_to_all | solution.py:37
  117.9 3.2 %gather_fusion = bf16[16,32,1536]{2,1,0:T(8,128)(2,1)} fusion(bf16[16,32,1536]{2,1,0:T(8,128)(2,1)} %all-to-all-done.1, s32[1024]{0:T(1024)S(1)} %pad_clamp_fusion), kind=kCustom, calls=%fused_computation | custom fusion | bytes 3145792 | tf_op jit(solution)/shard_map/jit(_take)/gather | solution.py:38
  121.1 2.8 %broadcast_select_fusion = bf16[16,32,1536]{2,1,0:T(8,128)(2,1)} fusion(bf16[16,32,1536]{2,1,0:T(8,128)(2,1)} %gather_fusion, pred[16]{0:T(512)(128)(4,1)S(1)} %compare_and_fusion), kind=kLoop, calls=%fused_computation.26 | loop fusion | flops 786432 | bytes 3145744 | tf_op jit(solution)/shard_map/jit(_take)/select_n | solution.py:38
  123.9 5.4 %all-to-all-start.2 = ((bf16[16,32,1536]{2,1,0:T(8,128)(2,1)}), bf16[16,32,1536]{2,1,0:T(8,128)(2,1)}, u32[]{:S(2)}, u32[]{:S(2)}) async-start(bf16[16,32,1536]{2,1,0:T(8,128)(2,1)} %broadcast_select_fusion), calls=%async_computation.3 | async-start | bytes 3145728 | tf_op jit(solution)/shard_map/all_to_all | solution.py:39
  129.3 35.6 %all-to-all-done.2 = bf16[16,32,1536]{2,1,0:T(8,128)(2,1)} async-done(((bf16[16,32,1536]{2,1,0:T(8,128)(2,1)}), bf16[16,32,1536]{2,1,0:T(8,128)(2,1)}, u32[]{:S(2)}, u32[]{:S(2)}) %all-to-all-start.2) | async-done | bytes 1572896 | tf_op jit(solution)/shard_map/all_to_all | solution.py:39
  164.9 5.4 %all-to-all-start = ((bf16[16,32,1024]{2,1,0:T(8,128)(2,1)}), bf16[16,32,1024]{2,1,0:T(8,128)(2,1)S(1)}, u32[]{:S(2)}, u32[]{:S(2)}) async-start(bf16[16,32,1024]{2,1,0:T(8,128)(2,1)} %bitcast.50), calls=%async_computation.1 | async-start | bytes 2097152 | tf_op jit(solution)/shard_map/all_to_all | solution.py:46
  170.3 0.1 reshape.58
  170.4 5.1 %convolution_bitcast_fusion.1 = f32[1,2048,512]{2,1,0:T(8,128)} fusion(bf16[2,512,2048]{2,1,0:T(8,128)(2,1)} %all-gather.4.cloned.1.call-done, bf16[512,1536]{1,0:T(8,128)(2,1)} %bitcast.11), kind=kOutput, calls=%fused_computation.8 | convolution fusion | flops 1073741824 | bytes 6815744 | tf_op jit(solution)/shard_map/dot_general | solution.py:53
  175.6 4.4 %convolution_bitcast_fusion.2 = f32[1,2048,512]{2,1,0:T(8,128)} fusion(bf16[2,512,2048]{2,1,0:T(8,128)(2,1)S(1)} %copy-done.2, bf16[512,1536]{1,0:T(8,128)(2,1)} %bitcast.11), kind=kOutput, calls=%fused_computation.9 | convolution fusion | flops 1073741824 | bytes 6815744 | tf_op jit(solution)/shard_map/dot_general | solution.py:50
  179.9 4.5 %convolution_bitcast_fusion = f32[1,2048,512]{2,1,0:T(8,128)} fusion(f32[512]{0:T(512)S(1)} %reshape.58, bf16[2,512,2048]{2,1,0:T(8,128)(2,1)S(1)} %copy-done.2, bf16[512,1536]{1,0:T(8,128)(2,1)} %bitcast.11), kind=kOutput, calls=%fused_computation.7 | convolution fusion | flops 1076887552 | bytes 6817792 | tf_op jit(solution)/shard_map/dot_general | solution.py:59
  184.4 10.9 %all-to-all-done = bf16[16,32,1024]{2,1,0:T(8,128)(2,1)S(1)} async-done(((bf16[16,32,1024]{2,1,0:T(8,128)(2,1)}), bf16[16,32,1024]{2,1,0:T(8,128)(2,1)S(1)}, u32[]{:S(2)}, u32[]{:S(2)}) %all-to-all-start) | async-done | bytes 1048608 | tf_op jit(solution)/shard_map/all_to_all | solution.py:46
  195.3 0.8 reduce_sum.31
  (14 shorter events, 0.1 us)
Async XLA Ops:
  7.2 65.0 %copy-start = (bf16[1,2048,512]{2,1,0:T(8,128)(2,1)S(1)}, bf16[1,2048,512]{2,1,0:T(8,128)(2,1)}, u32[]{:S(2)}) copy-start(bf16[1,2048,512]{2,1,0:T(8,128)(2,1)} %param.14) | copy-start | bytes 6291460
  7.2 59.5 %all-gather.4.cloned.1.call-start = ((), (), s32[]{:S(2)}) async-start(), calls=%async_computation.4 | async-start | bytes 4456448 | tf_op jit(solution)/shard_map/all_gather | solution.py:25
  66.7 3.7 %copy-start.1 = (bf16[2,512,2048]{2,1,0:T(8,128)(2,1)S(1)}, bf16[2,512,2048]{2,1,0:T(8,128)(2,1)}, u32[]{:S(2)}) copy-start(bf16[2,512,2048]{2,1,0:T(8,128)(2,1)} %all-gather.4.cloned.1.call-done) | copy-start | bytes 12582916
  66.7 4.1 %copy-start.3 = (bf16[1,2048,512]{2,1,0:T(8,128)(2,1)S(1)}, bf16[1,2048,512]{2,1,0:T(8,128)(2,1)}, u32[]{:S(2)}) copy-start(bf16[1,2048,512]{2,1,0:T(8,128)(2,1)} %param.15) | copy-start | bytes 6291460
  77.7 40.2 %all-to-all-start.1 = ((bf16[16,32,1536]{2,1,0:T(8,128)(2,1)}), bf16[16,32,1536]{2,1,0:T(8,128)(2,1)}, u32[]{:S(2)}, u32[]{:S(2)}) async-start(bf16[16,32,1536]{2,1,0:T(8,128)(2,1)} %bitcast.49), calls=%async_computation.2 | async-start | bytes 3145728 | tf_op jit(solution)/shard_map/all_to_all | solution.py:37
  82.2 47.1 %reduce-scatter.2.cloned.1.call-start = ((), (), s32[]{:S(2)}) async-start(), calls=%async_computation.5 | async-start | bytes 3145728 | tf_op jit(solution)/shard_map/reduce_scatter | solution.py:44
  87.8 0.7 copy-start.4
  123.9 41.1 %all-to-all-start.2 = ((bf16[16,32,1536]{2,1,0:T(8,128)(2,1)}), bf16[16,32,1536]{2,1,0:T(8,128)(2,1)}, u32[]{:S(2)}, u32[]{:S(2)}) async-start(bf16[16,32,1536]{2,1,0:T(8,128)(2,1)} %broadcast_select_fusion), calls=%async_computation.3 | async-start | bytes 3145728 | tf_op jit(solution)/shard_map/all_to_all | solution.py:39
  164.9 30.3 %all-to-all-start = ((bf16[16,32,1024]{2,1,0:T(8,128)(2,1)}), bf16[16,32,1024]{2,1,0:T(8,128)(2,1)S(1)}, u32[]{:S(2)}, u32[]{:S(2)}) async-start(bf16[16,32,1024]{2,1,0:T(8,128)(2,1)} %bitcast.50), calls=%async_computation.1 | async-start | bytes 2097152 | tf_op jit(solution)/shard_map/all_to_all | solution.py:46
  170.4 5.1 %copy-start.2 = (bf16[2,512,2048]{2,1,0:T(8,128)(2,1)S(1)}, bf16[2,512,2048]{2,1,0:T(8,128)(2,1)}, u32[]{:S(2)}) copy-start(bf16[2,512,2048]{2,1,0:T(8,128)(2,1)} %all-gather.4.cloned.1.call-done) | copy-start | bytes 12582916
Sparse Core Ops, SparseCore 0:
  13.5 53.0 all-gather.3
  88.0 32.3 reduce-scatter.1
where the time goes:
time: 204 us; the launch traced here: 203 us
  waiting for transfers between devices  87.9 us (43%)
  blocking collectives  44.5 us (22%)
  matrix products  26.2 us (13%)
  starting transfers between devices  15.4 us (8%)
  between operations  14.1 us (7%)
  local copies, waits for them, and re-layouts  8.26 us (4%)
  other arithmetic  6.57 us (3%)
    all_to_all x1, waiting for transfers between devices, local(): lax.all_to_all(ordered, 'expert', split_axis=0, concat_axis=0, tiled=True)  35.6 us
    all_to_all x1, waiting for transfers between devices, local(): lax.all_to_all(packed, 'expert', split_axis=0, concat_axis=0, tiled=True)  29.4 us
    all_gather x1, blocking collectives, local(): routes_all = lax.all_gather(routes, 'expert', axis=0, tiled=True)  20.8 us
    all_gather x1, blocking collectives, local(): probs_all = lax.all_gather(probs, 'expert', axis=0, tiled=True)  18.5 us
    all_gather x1, waiting for transfers between devices, local(): both = lax.all_gather(both, 'expert', axis=1, tiled=True)  11.9 us
    all_to_all x1, waiting for transfers between devices, local(): lax.all_to_all(summed, 'expert', split_axis=0, concat_axis=0, tiled=True)  10.9 us
    all_to_all x1, starting transfers between devices, local(): lax.all_to_all(ordered, 'expert', split_axis=0, concat_axis=0, tiled=True)  5.42 us
    all_to_all x1, starting transfers between devices, local(): lax.all_to_all(summed, 'expert', split_axis=0, concat_axis=0, tiled=True)  5.41 us
  transfers between devices with their start and end apart: 5, of which 4 were waited for; matrix products, arithmetic and copies ran while one was open for 14% of the time, Pallas kernels for 0%

commit v1 on v0

--- a/solution.py
+++ b/solution.py
@@ -19,7 +19,14 @@
     me = lax.axis_index("expert")
     w_gate, w_up, w_down = (gate_weight[0], up_weight[0], down_weight[0])
     routes_all = lax.all_gather(routes, "expert", axis=0, tiled=True)
-    probs_all = lax.all_gather(probs, "expert", axis=0, tiled=True)
+    ring = [probs]
+    for hop in range(15):
+        ring.append(lax.ppermute(ring[-1], "expert", [(dev, (dev + 1) % 16) for dev in range(16)]))
+    probs_all = jnp.roll(
+        jnp.concatenate(ring[::-1], axis=0),
+        (lax.axis_index("expert") + 1) * ring[0].shape[0],
+        axis=0,
+    )
     both = jnp.stack([tokens, cotangent], axis=0)
     both = lax.all_gather(both, "dp", axis=2, tiled=True)
     both = lax.all_gather(both, "expert", axis=1, tiled=True)

time: 204 us -> 253 us (1.24)
  waiting for transfers between devices: 87.9 us -> 119 us
  starting transfers between devices: 15.4 us -> 36.7 us
    ppermute x0 -> x15, waiting for transfers between devices: none -> 41.3 us  [local(): lax.ppermute(ring[-1], 'expert', [(dev, (dev + 1) % 16) for dev in range(...]
    all_gather x1 -> x0, blocking collectives: 18.5 us -> none  [local(): probs_all = lax.all_gather(probs, 'expert', axis=0, tiled=True)]
    all_gather x1, blocking collectives: 20.8 us -> 37 us  [local(): routes_all = lax.all_gather(routes, 'expert', axis=0, tiled=True)]
    ppermute x0 -> x15, starting transfers between devices: none -> 13.2 us  [local(): lax.ppermute(ring[-1], 'expert', [(dev, (dev + 1) % 16) for dev in range(...]
    all_gather x1, waiting for transfers between devices: 11.9 us -> 0.02 us  [local(): both = lax.all_gather(both, 'expert', axis=1, tiled=True)]
    all_to_all x1, starting transfers between devices: 4.52 us -> 12.7 us  [local(): lax.all_to_all(packed, 'expert', split_axis=0, concat_axis=0, tiled=True)]
  transfers between devices with their start and end apart: 5 -> 20, of which waited for: 4 -> 17; matrix products, arithmetic and copies ran while one was open for 14% -> 11% of each run, Pallas kernels for 0% -> 0%
where the time goes in v1:
time: 253 us; the launch traced here: 252 us
  waiting for transfers between devices  119 us (47%)
  blocking collectives  42.1 us (17%)
  starting transfers between devices  36.7 us (15%)
  matrix products  24 us (9%)
  between operations  14.2 us (6%)
  local copies, waits for them, and re-layouts  9.69 us (4%)
  other arithmetic  6.64 us (3%)
    ppermute x15, waiting for transfers between devices, local(): lax.ppermute(ring[-1], 'expert', [(dev, (dev + 1) % 16) for dev in range(...  41.3 us
    all_gather x1, blocking collectives, local(): routes_all = lax.all_gather(routes, 'expert', axis=0, tiled=True)  37 us
    all_to_all x1, waiting for transfers between devices, local(): lax.all_to_all(ordered, 'expert', split_axis=0, concat_axis=0, tiled=True)  35.6 us
    all_to_all x1, waiting for transfers between devices, local(): lax.all_to_all(packed, 'expert', split_axis=0, concat_axis=0, tiled=True)  30.7 us
    ppermute x15, starting transfers between devices, local(): lax.ppermute(ring[-1], 'expert', [(dev, (dev + 1) % 16) for dev in range(...  13.2 us
    all_to_all x1, starting transfers between devices, local(): lax.all_to_all(packed, 'expert', split_axis=0, concat_axis=0, tiled=True)  12.7 us
    all_to_all x1, waiting for transfers between devices, local(): lax.all_to_all(summed, 'expert', split_axis=0, concat_axis=0, tiled=True)  11 us
    all_to_all x1, starting transfers between devices, local(): lax.all_to_all(summed, 'expert', split_axis=0, concat_axis=0, tiled=True)  5.41 us
  transfers between devices with their start and end apart: 20, of which 17 were waited for; matrix products, arithmetic and copies ran while one was open for 11% of the time, Pallas kernels for 0%

profile of v1, /device:TPU:9, one launch (start us, length us, event | category | flops | bytes accessed | tf_op | source)
XLA Modules:
  0.0 252.0 jit_solution(179990245700705415)
XLA Ops:
  8.3 5.1 %all_gather.9 = bf16[2,32,2048]{2,1,0:T(8,128)(2,1)} all-gather(bf16[2,32,1024]{2,1,0:T(8,128)(2,1)S(1)} %pad_maximum_fusion.1), channel_id=1, replica_groups=mesh['dp'=2,'expert'=16] {'dp'}, dimensions={2}, use_global_device_ids=true | all-gather | bytes 393216 | tf_op jit(solution)/shard_map/all_gather | solution.py:31
  13.4 2.7 %collective-permute-start = (f32[32,8]{0,1:T(8,128)}, f32[32,8]{0,1:T(8,128)S(1)}, u32[]{:S(2)}, u32[]{:S(2)}) collective-permute-start(f32[32,8]{0,1:T(8,128)} %param.11), channel_id=1, source_target_pairs={{0,1},{1,2},{2,3},{3,4},{4,5},{5,6},{6,7},{7,8},{8,9},{9,10},{10,1... | collective-permute-start | bytes 3080 | tf_op jit(solution)/shard_map/ppermute | solution.py:24
  17.1 2.3 collective-permute-start.1
  20.1 2.3 collective-permute-start.2
  23.7 1.7 collective-permute-start.3
  25.4 2.3 collective-permute-done.3
  28.5 3.2 %collective-permute-done.4 = f32[32,8]{0,1:T(8,128)S(1)} collective-permute-done((f32[32,8]{0,1:T(8,128)S(1)}, f32[32,8]{0,1:T(8,128)S(1)}, u32[]{:S(2)}, u32[]{:S(2)}) %collective-permute-start.4) | collective-permute-done | bytes 1056 | tf_op jit(solution)/shard_map/ppermute | solution.py:24
  31.8 3.9 %collective-permute-done.5 = f32[32,8]{0,1:T(8,128)S(1)} collective-permute-done((f32[32,8]{0,1:T(8,128)S(1)}, f32[32,8]{0,1:T(8,128)S(1)}, u32[]{:S(2)}, u32[]{:S(2)}) %collective-permute-start.5) | collective-permute-done | bytes 1056 | tf_op jit(solution)/shard_map/ppermute | solution.py:24
  35.7 3.9 %collective-permute-done.6 = f32[32,8]{0,1:T(8,128)S(1)} collective-permute-done((f32[32,8]{0,1:T(8,128)S(1)}, f32[32,8]{0,1:T(8,128)S(1)}, u32[]{:S(2)}, u32[]{:S(2)}) %collective-permute-start.6) | collective-permute-done | bytes 1056 | tf_op jit(solution)/shard_map/ppermute | solution.py:24
  39.6 3.9 %collective-permute-done.7 = f32[32,8]{0,1:T(8,128)S(1)} collective-permute-done((f32[32,8]{0,1:T(8,128)S(1)}, f32[32,8]{0,1:T(8,128)S(1)}, u32[]{:S(2)}, u32[]{:S(2)}) %collective-permute-start.7) | collective-permute-done | bytes 1056 | tf_op jit(solution)/shard_map/ppermute | solution.py:24
  43.6 4.1 %collective-permute-done.8 = f32[32,8]{0,1:T(8,128)S(1)} collective-permute-done((f32[32,8]{0,1:T(8,128)S(1)}, f32[32,8]{0,1:T(8,128)S(1)}, u32[]{:S(2)}, u32[]{:S(2)}) %collective-permute-start.8) | collective-permute-done | bytes 1056 | tf_op jit(solution)/shard_map/ppermute | solution.py:24
  47.6 4.1 %collective-permute-done.9 = f32[32,8]{0,1:T(8,128)S(1)} collective-permute-done((f32[32,8]{0,1:T(8,128)S(1)}, f32[32,8]{0,1:T(8,128)S(1)}, u32[]{:S(2)}, u32[]{:S(2)}) %collective-permute-start.9) | collective-permute-done | bytes 1056 | tf_op jit(solution)/shard_map/ppermute | solution.py:24
  51.8 5.0 %collective-permute-done.10 = f32[32,8]{0,1:T(8,128)S(1)} collective-permute-done((f32[32,8]{0,1:T(8,128)S(1)}, f32[32,8]{0,1:T(8,128)S(1)}, u32[]{:S(2)}, u32[]{:S(2)}) %collective-permute-start.10) | collective-permute-done | bytes 1056 | tf_op jit(solution)/shard_map/ppermute | solution.py:24
  56.8 5.8 %collective-permute-done.11 = f32[32,8]{0,1:T(8,128)S(1)} collective-permute-done((f32[32,8]{0,1:T(8,128)S(1)}, f32[32,8]{0,1:T(8,128)S(1)}, u32[]{:S(2)}, u32[]{:S(2)}) %collective-permute-start.11) | collective-permute-done | bytes 1056 | tf_op jit(solution)/shard_map/ppermute | solution.py:24
  62.7 37.0 %all-gather = s32[16,32,8]{1,2,0:T(8,128)S(1)} all-gather(s32[1,32,8]{1,2,0:T(8,128)} %bitcast.56), channel_id=1, replica_groups=mesh['dp'=2,'expert'=16] {'expert'}, dimensions={0}, use_global_device_ids=true | all-gather | bytes 17408 | tf_op jit(solution)/shard_map/all_gather | solution.py:21
  102.8 2.3 collective-permute-start.14
  105.3 1.7 collective-permute-done.14
  108.0 3.0 %fusion.9 = f32[512,512]{0,1:T(8,128)S(1)} fusion(bf16[1,2048,512]{2,1,0:T(8,128)(2,1)S(1)} %copy-done, bf16[2,512,2048]{2,1,0:T(8,128)(2,1)} %all-gather.3.cloned.1.call-done), kind=kOutput, calls=%fused_computation.15 | convolution fusion | flops 1073741824 | bytes 5242880 | tf_op jit(solution)/shard_map/dot_general | solution.py:35
  113.1 1.7 multiply_convert_fusion
  116.1 2.6 %copy.19 = bf16[512,1536]{1,0:T(8,128)(2,1)} copy(bf16[512,1536]{0,1:T(8,128)(2,1)} %pad_maximum_fusion) | data formatting | bytes 3145728 | tf_op jit(solution)/shard_map/concatenate | solution.py:42
  118.6 12.7 %all-to-all-start.1 = ((bf16[16,32,1536]{2,1,0:T(8,128)(2,1)}), bf16[16,32,1536]{2,1,0:T(8,128)(2,1)}, u32[]{:S(2)}, u32[]{:S(2)}) async-start(bf16[16,32,1536]{2,1,0:T(8,128)(2,1)} %bitcast.52), calls=%async_computation.2 | async-start | bytes 3145728 | tf_op jit(solution)/shard_map/all_to_all | solution.py:44
  133.0 2.6 %add_convert_fusion = bf16[512,2048]{1,0:T(8,128)(2,1)} fusion(f32[512,2048]{1,0:T(8,128)S(1)} %fusion.7, bf16[512,512]{0,1:T(8,128)(2,1)S(1)} %get-tuple-element.8, bf16[1,2048,512]{2,1,0:T(8,128)(2,1)S(1)} %copy-done.2), kind=kOutput, calls=%fused_computation.6 | convolution fusion | flops 1075838976 | bytes 8912896 | tf_op jit(solution)/shard_map/dot_general | solution.py:49
  136.3 30.7 %all-to-all-done.1 = bf16[16,32,1536]{2,1,0:T(8,128)(2,1)} async-done(((bf16[16,32,1536]{2,1,0:T(8,128)(2,1)}), bf16[16,32,1536]{2,1,0:T(8,128)(2,1)}, u32[]{:S(2)}, u32[]{:S(2)}) %all-to-all-start.1) | async-done | bytes 1572896 | tf_op jit(solution)/shard_map/all_to_all | solution.py:44
  167.0 3.2 %gather_fusion = bf16[16,32,1536]{2,1,0:T(8,128)(2,1)} fusion(bf16[16,32,1536]{2,1,0:T(8,128)(2,1)} %all-to-all-done.1, s32[1024]{0:T(1024)S(1)} %pad_clamp_fusion), kind=kCustom, calls=%fused_computation | custom fusion | bytes 3145792 | tf_op jit(solution)/shard_map/jit(_take)/gather | solution.py:45
  170.2 2.8 %broadcast_select_fusion = bf16[16,32,1536]{2,1,0:T(8,128)(2,1)} fusion(bf16[16,32,1536]{2,1,0:T(8,128)(2,1)} %gather_fusion, pred[16]{0:T(512)(128)(4,1)S(1)} %compare_and_fusion), kind=kLoop, calls=%fused_computation.26 | loop fusion | flops 786432 | bytes 3145744 | tf_op jit(solution)/shard_map/jit(_take)/select_n | solution.py:45
  173.0 5.4 %all-to-all-start.2 = ((bf16[16,32,1536]{2,1,0:T(8,128)(2,1)}), bf16[16,32,1536]{2,1,0:T(8,128)(2,1)}, u32[]{:S(2)}, u32[]{:S(2)}) async-start(bf16[16,32,1536]{2,1,0:T(8,128)(2,1)} %broadcast_select_fusion), calls=%async_computation.3 | async-start | bytes 3145728 | tf_op jit(solution)/shard_map/all_to_all | solution.py:46
  178.4 35.6 %all-to-all-done.2 = bf16[16,32,1536]{2,1,0:T(8,128)(2,1)} async-done(((bf16[16,32,1536]{2,1,0:T(8,128)(2,1)}), bf16[16,32,1536]{2,1,0:T(8,128)(2,1)}, u32[]{:S(2)}, u32[]{:S(2)}) %all-to-all-start.2) | async-done | bytes 1572896 | tf_op jit(solution)/shard_map/all_to_all | solution.py:46
  214.0 5.4 %all-to-all-start = ((bf16[16,32,1024]{2,1,0:T(8,128)(2,1)}), bf16[16,32,1024]{2,1,0:T(8,128)(2,1)S(1)}, u32[]{:S(2)}, u32[]{:S(2)}) async-start(bf16[16,32,1024]{2,1,0:T(8,128)(2,1)} %bitcast.53), calls=%async_computation.1 | async-start | bytes 2097152 | tf_op jit(solution)/shard_map/all_to_all | solution.py:53
  219.4 5.1 %convolution_bitcast_fusion.1 = f32[1,2048,512]{2,1,0:T(8,128)} fusion(bf16[2,512,2048]{2,1,0:T(8,128)(2,1)} %all-gather.3.cloned.1.call-done, bf16[512,1536]{1,0:T(8,128)(2,1)} %bitcast.10), kind=kOutput, calls=%fused_computation.8 | convolution fusion | flops 1073741824 | bytes 6815744 | tf_op jit(solution)/shard_map/dot_general | solution.py:60
  224.6 4.4 %convolution_bitcast_fusion.2 = f32[1,2048,512]{2,1,0:T(8,128)} fusion(bf16[2,512,2048]{2,1,0:T(8,128)(2,1)S(1)} %copy-done.4, bf16[512,1536]{1,0:T(8,128)(2,1)} %bitcast.10), kind=kOutput, calls=%fused_computation.9 | convolution fusion | flops 1073741824 | bytes 6815744 | tf_op jit(solution)/shard_map/dot_general | solution.py:57
  228.9 4.5 %convolution_bitcast_fusion = f32[1,2048,512]{2,1,0:T(8,128)} fusion(f32[512]{0:T(512)S(1)} %get-tuple-element.4, bf16[2,512,2048]{2,1,0:T(8,128)(2,1)S(1)} %copy-done.4, bf16[512,1536]{1,0:T(8,128)(2,1)} %bitcast.10), kind=kOutput, calls=%fused_computation.7 | convolution fusion | flops 1076887552 | bytes 6817792 | tf_op jit(solution)/shard_map/dot_general | solution.py:66
  233.4 11.0 %all-to-all-done = bf16[16,32,1024]{2,1,0:T(8,128)(2,1)S(1)} async-done(((bf16[16,32,1024]{2,1,0:T(8,128)(2,1)}), bf16[16,32,1024]{2,1,0:T(8,128)(2,1)S(1)}, u32[]{:S(2)}, u32[]{:S(2)}) %all-to-all-start) | async-done | bytes 1048608 | tf_op jit(solution)/shard_map/all_to_all | solution.py:53
  (51 shorter events, 15.6 us)
Async XLA Ops:
  7.2 100.8 %copy-start = (bf16[1,2048,512]{2,1,0:T(8,128)(2,1)S(1)}, bf16[1,2048,512]{2,1,0:T(8,128)(2,1)}, u32[]{:S(2)}) copy-start(bf16[1,2048,512]{2,1,0:T(8,128)(2,1)} %param.13) | copy-start | bytes 6291460
  7.2 100.8 %all-gather.3.cloned.1.call-start = ((), (), s32[]{:S(2)}) async-start(), calls=%async_computation.4 | async-start | bytes 4456448 | tf_op jit(solution)/shard_map/all_gather | solution.py:32
  13.4 3.7 %collective-permute-start = (f32[32,8]{0,1:T(8,128)}, f32[32,8]{0,1:T(8,128)S(1)}, u32[]{:S(2)}, u32[]{:S(2)}) collective-permute-start(f32[32,8]{0,1:T(8,128)} %param.11), channel_id=1, source_target_pairs={{0,1},{1,2},{2,3},{3,4},{4,5},{5,6},{6,7},{7,8},{8,9},{9,10},{10,1... | collective-permute-start | bytes 3080 | tf_op jit(solution)/shard_map/ppermute | solution.py:24
  17.1 3.0 %collective-permute-start.1 = (f32[32,8]{0,1:T(8,128)S(1)}, f32[32,8]{0,1:T(8,128)S(1)}, u32[]{:S(2)}, u32[]{:S(2)}) collective-permute-start(f32[32,8]{0,1:T(8,128)S(1)} %collective-permute-done), channel_id=1, source_target_pairs={{0,1},{1,2},{2,3},{3,4},{4,5},{5,6},{6,7},{7,8},{8,9},{9,10},{10,1... | collective-permute-start | bytes 3080 | tf_op jit(solution)/shard_map/ppermute | solution.py:24
  20.1 3.6 %collective-permute-start.2 = (f32[32,8]{0,1:T(8,128)S(1)}, f32[32,8]{0,1:T(8,128)S(1)}, u32[]{:S(2)}, u32[]{:S(2)}) collective-permute-start(f32[32,8]{0,1:T(8,128)S(1)} %collective-permute-done.1), channel_id=1, source_target_pairs={{0,1},{1,2},{2,3},{3,4},{4,5},{5,6},{6,7},{7,8},{8,9},{9,10},{10,1... | collective-permute-start | bytes 3080 | tf_op jit(solution)/shard_map/ppermute | solution.py:24
  23.7 4.0 %collective-permute-start.3 = (f32[32,8]{0,1:T(8,128)S(1)}, f32[32,8]{0,1:T(8,128)S(1)}, u32[]{:S(2)}, u32[]{:S(2)}) collective-permute-start(f32[32,8]{0,1:T(8,128)S(1)} %collective-permute-done.2), channel_id=1, source_target_pairs={{0,1},{1,2},{2,3},{3,4},{4,5},{5,6},{6,7},{7,8},{8,9},{9,10},{10,1... | collective-permute-start | bytes 3080 | tf_op jit(solution)/shard_map/ppermute | solution.py:24
  27.8 4.0 %collective-permute-start.4 = (f32[32,8]{0,1:T(8,128)S(1)}, f32[32,8]{0,1:T(8,128)S(1)}, u32[]{:S(2)}, u32[]{:S(2)}) collective-permute-start(f32[32,8]{0,1:T(8,128)S(1)} %collective-permute-done.3), channel_id=1, source_target_pairs={{0,1},{1,2},{2,3},{3,4},{4,5},{5,6},{6,7},{7,8},{8,9},{9,10},{10,1... | collective-permute-start | bytes 3080 | tf_op jit(solution)/shard_map/ppermute | solution.py:24
  31.8 3.9 %collective-permute-start.5 = (f32[32,8]{0,1:T(8,128)S(1)}, f32[32,8]{0,1:T(8,128)S(1)}, u32[]{:S(2)}, u32[]{:S(2)}) collective-permute-start(f32[32,8]{0,1:T(8,128)S(1)} %collective-permute-done.4), channel_id=1, source_target_pairs={{0,1},{1,2},{2,3},{3,4},{4,5},{5,6},{6,7},{7,8},{8,9},{9,10},{10,1... | collective-permute-start | bytes 3080 | tf_op jit(solution)/shard_map/ppermute | solution.py:24
  35.7 3.9 %collective-permute-start.6 = (f32[32,8]{0,1:T(8,128)S(1)}, f32[32,8]{0,1:T(8,128)S(1)}, u32[]{:S(2)}, u32[]{:S(2)}) collective-permute-start(f32[32,8]{0,1:T(8,128)S(1)} %collective-permute-done.5), channel_id=1, source_target_pairs={{0,1},{1,2},{2,3},{3,4},{4,5},{5,6},{6,7},{7,8},{8,9},{9,10},{10,1... | collective-permute-start | bytes 3080 | tf_op jit(solution)/shard_map/ppermute | solution.py:24
  39.6 3.9 %collective-permute-start.7 = (f32[32,8]{0,1:T(8,128)S(1)}, f32[32,8]{0,1:T(8,128)S(1)}, u32[]{:S(2)}, u32[]{:S(2)}) collective-permute-start(f32[32,8]{0,1:T(8,128)S(1)} %collective-permute-done.6), channel_id=1, source_target_pairs={{0,1},{1,2},{2,3},{3,4},{4,5},{5,6},{6,7},{7,8},{8,9},{9,10},{10,1... | collective-permute-start | bytes 3080 | tf_op jit(solution)/shard_map/ppermute | solution.py:24
  43.6 4.1 %collective-permute-start.8 = (f32[32,8]{0,1:T(8,128)S(1)}, f32[32,8]{0,1:T(8,128)S(1)}, u32[]{:S(2)}, u32[]{:S(2)}) collective-permute-start(f32[32,8]{0,1:T(8,128)S(1)} %collective-permute-done.7), channel_id=1, source_target_pairs={{0,1},{1,2},{2,3},{3,4},{4,5},{5,6},{6,7},{7,8},{8,9},{9,10},{10,1... | collective-permute-start | bytes 3080 | tf_op jit(solution)/shard_map/ppermute | solution.py:24
  47.6 4.1 %collective-permute-start.9 = (f32[32,8]{0,1:T(8,128)S(1)}, f32[32,8]{0,1:T(8,128)S(1)}, u32[]{:S(2)}, u32[]{:S(2)}) collective-permute-start(f32[32,8]{0,1:T(8,128)S(1)} %collective-permute-done.8), channel_id=1, source_target_pairs={{0,1},{1,2},{2,3},{3,4},{4,5},{5,6},{6,7},{7,8},{8,9},{9,10},{10,1... | collective-permute-start | bytes 3080 | tf_op jit(solution)/shard_map/ppermute | solution.py:24
  51.8 5.0 %collective-permute-start.10 = (f32[32,8]{0,1:T(8,128)S(1)}, f32[32,8]{0,1:T(8,128)S(1)}, u32[]{:S(2)}, u32[]{:S(2)}) collective-permute-start(f32[32,8]{0,1:T(8,128)S(1)} %collective-permute-done.9), channel_id=1, source_target_pairs={{0,1},{1,2},{2,3},{3,4},{4,5},{5,6},{6,7},{7,8},{8,9},{9,10},{10,1... | collective-permute-start | bytes 3080 | tf_op jit(solution)/shard_map/ppermute | solution.py:24
  56.8 5.8 %collective-permute-start.11 = (f32[32,8]{0,1:T(8,128)S(1)}, f32[32,8]{0,1:T(8,128)S(1)}, u32[]{:S(2)}, u32[]{:S(2)}) collective-permute-start(f32[32,8]{0,1:T(8,128)S(1)} %collective-permute-done.10), channel_id=1, source_target_pairs={{0,1},{1,2},{2,3},{3,4},{4,5},{5,6},{6,7},{7,8},{8,9},{9,10},{10,1... | collective-permute-start | bytes 3080 | tf_op jit(solution)/shard_map/ppermute | solution.py:24
  62.7 38.2 %collective-permute-start.12 = (f32[32,8]{0,1:T(8,128)S(1)}, f32[32,8]{0,1:T(8,128)S(1)}, u32[]{:S(2)}, u32[]{:S(2)}) collective-permute-start(f32[32,8]{0,1:T(8,128)S(1)} %collective-permute-done.11), channel_id=1, source_target_pairs={{0,1},{1,2},{2,3},{3,4},{4,5},{5,6},{6,7},{7,8},{8,9},{9,10},{10,1... | collective-permute-start | bytes 3080 | tf_op jit(solution)/shard_map/ppermute | solution.py:24
  100.9 1.9 collective-permute-start.13
  102.8 4.2 %collective-permute-start.14 = (f32[32,8]{0,1:T(8,128)S(1)}, f32[32,8]{0,1:T(8,128)S(1)}, u32[]{:S(2)}, u32[]{:S(2)}) collective-permute-start(f32[32,8]{0,1:T(8,128)S(1)} %collective-permute-done.13), channel_id=1, source_target_pairs={{0,1},{1,2},{2,3},{3,4},{4,5},{5,6},{6,7},{7,8},{8,9},{9,10},{10,1... | collective-permute-start | bytes 3080 | tf_op jit(solution)/shard_map/ppermute | solution.py:24
  108.0 3.1 %copy-start.1 = (bf16[1,2048,512]{2,1,0:T(8,128)(2,1)S(1)}, bf16[1,2048,512]{2,1,0:T(8,128)(2,1)}, u32[]{:S(2)}) copy-start(bf16[1,2048,512]{2,1,0:T(8,128)(2,1)} %param.14) | copy-start | bytes 6291460
  108.0 3.4 %copy-start.3 = (bf16[2,512,2048]{2,1,0:T(8,128)(2,1)S(1)}, bf16[2,512,2048]{2,1,0:T(8,128)(2,1)}, u32[]{:S(2)}) copy-start(bf16[2,512,2048]{2,1,0:T(8,128)(2,1)} %all-gather.3.cloned.1.call-done) | copy-start | bytes 12582916
  111.5 1.6 copy-start.5
  118.6 48.4 %all-to-all-start.1 = ((bf16[16,32,1536]{2,1,0:T(8,128)(2,1)}), bf16[16,32,1536]{2,1,0:T(8,128)(2,1)}, u32[]{:S(2)}, u32[]{:S(2)}) async-start(bf16[16,32,1536]{2,1,0:T(8,128)(2,1)} %bitcast.52), calls=%async_computation.2 | async-start | bytes 3145728 | tf_op jit(solution)/shard_map/all_to_all | solution.py:44
  131.3 47.0 %reduce-scatter.2.cloned.1.call-start = ((), (), s32[]{:S(2)}) async-start(), calls=%async_computation.5 | async-start | bytes 3145728 | tf_op jit(solution)/shard_map/reduce_scatter | solution.py:51
  131.4 1.6 copy-start.2
  135.6 0.7 copy-start.6
  173.0 41.0 %all-to-all-start.2 = ((bf16[16,32,1536]{2,1,0:T(8,128)(2,1)}), bf16[16,32,1536]{2,1,0:T(8,128)(2,1)}, u32[]{:S(2)}, u32[]{:S(2)}) async-start(bf16[16,32,1536]{2,1,0:T(8,128)(2,1)} %broadcast_select_fusion), calls=%async_computation.3 | async-start | bytes 3145728 | tf_op jit(solution)/shard_map/all_to_all | solution.py:46
  214.0 30.3 %all-to-all-start = ((bf16[16,32,1024]{2,1,0:T(8,128)(2,1)}), bf16[16,32,1024]{2,1,0:T(8,128)(2,1)S(1)}, u32[]{:S(2)}, u32[]{:S(2)}) async-start(bf16[16,32,1024]{2,1,0:T(8,128)(2,1)} %bitcast.53), calls=%async_computation.1 | async-start | bytes 2097152 | tf_op jit(solution)/shard_map/all_to_all | solution.py:53
  219.4 5.1 %copy-start.4 = (bf16[2,512,2048]{2,1,0:T(8,128)(2,1)S(1)}, bf16[2,512,2048]{2,1,0:T(8,128)(2,1)}, u32[]{:S(2)}) copy-start(bf16[2,512,2048]{2,1,0:T(8,128)(2,1)} %all-gather.3.cloned.1.call-done) | copy-start | bytes 12582916
Sparse Core Ops, SparseCore 0:
  13.5 53.0 all-gather.2
  135.7 32.5 reduce-scatter.1
